TPU v7x, 256 devices: a whole 4x4x8 slice. The times are simulated.
256 devices in a mesh: frame: 16 (over z_hi, y), space: 16 (over z_lo, x, core).
Axes of the slice: x: 4, y: 4, z: 8 (z_hi: 4, z_lo: 2; z = z_hi * 2 + z_lo), core: 2. Of those that a mesh axis runs over, the one named last changes fastest.
Arguments:
- hidden_in: bfloat16 [2, 16, 32, 64, 1152], P(None, 'frame', 'space'), may hold values from -6 to 6
- attn_cotangent: bfloat16 [2, 16, 32, 64, 1152], P(None, 'frame', 'space'), may hold values from -6 to 6
- w_qkv: bfloat16 [1152, 3456], P('space'), may hold values from -0.1875 to 0.1875
- modulation_table: bfloat16 [1000, 2, 1152], replicated, may hold values from -3 to 3
- snr_table: float32 [1000], replicated, may hold values from 0.1 to 1
- timestep: int32 [2], replicated, may hold values from 0 to 999
- weight_index: int32 [2], replicated, may hold values from 0 to 999
Outputs:
- grad_input: bfloat16 [2, 16, 32, 64, 1152], P(None, 'frame', 'space')
- grad_w_qkv: float32 [1152, 3456], P('space')
- grad_modulation: float32 [2, 2, 1152], replicated
All inputs are finite; a program needn't handle non-finite values.
Results may differ from a plain program's by a relative error of at most 0.029.
Values may be sent and summed in bfloat16 or wider, within the bound.
A program may use at most 128 MiB of HBM per device.

v0:
```python
import jax
import jax.numpy as jnp
from jax import lax
from jax.sharding import PartitionSpec as P

HEADS = 16
HEAD_DIM = 72


def attend_back(queries, keys, values, upstream):
    factor = queries.shape[-1] ** (-0.5)
    queries = queries.astype(jnp.float32)
    keys = keys.astype(jnp.float32)
    values = values.astype(jnp.float32)
    upstream = upstream.astype(jnp.float32)
    highest = lax.Precision.HIGHEST
    scores = jnp.einsum("bfxhe,bgxhe->bxhfg", queries, keys, precision=highest) * factor
    expd = jnp.exp(scores)
    probs = expd / jnp.sum(expd, axis=-1, keepdims=True)
    grad_probs = jnp.einsum("bfxhe,bgxhe->bxhfg", upstream, values, precision=highest)
    grad_values = jnp.einsum("bxhfg,bfxhe->bgxhe", probs, upstream, precision=highest)
    grad_scores = probs * (grad_probs - jnp.sum(probs * grad_probs, axis=-1, keepdims=True))
    grad_queries = jnp.einsum("bxhfg,bgxhe->bfxhe", grad_scores, keys, precision=highest) * factor
    grad_keys = jnp.einsum("bxhfg,bfxhe->bgxhe", grad_scores, queries, precision=highest) * factor
    return (
        grad_queries.astype(jnp.bfloat16),
        grad_keys.astype(jnp.bfloat16),
        grad_values.astype(jnp.bfloat16),
    )


def per_device(
    hidden_in, attn_cotangent, w_qkv, modulation_table, snr_table, timestep, weight_index
):
    clip_count, frame_dev, row_dev, col_count, model_width = hidden_in.shape
    positions = row_dev * col_count
    values_in = hidden_in.astype(jnp.float32)
    average = jnp.mean(values_in, axis=-1, keepdims=True)
    centered = values_in - average
    variance = jnp.mean(centered * centered, axis=-1, keepdims=True)
    inverse_std = lax.rsqrt(variance + 1e-06)
    normed = centered * inverse_std
    modulation = modulation_table[timestep].astype(jnp.float32)
    shift = modulation[:, 0][:, None, None, None, :]
    scale = modulation[:, 1][:, None, None, None, :]
    modulated = (normed * (1.0 + scale) + shift).astype(jnp.bfloat16)
    mod_rows = modulated.reshape(-1, model_width)
    w_full = lax.all_gather(w_qkv, "space", axis=0, tiled=True)
    projected = jnp.dot(mod_rows, w_full, preferred_element_type=jnp.float32).astype(jnp.bfloat16)
    projected = projected.reshape(clip_count, frame_dev, positions, 3, model_width)
    loss_weight = snr_table[weight_index]
    upstream = (loss_weight[:, None, None, None, None] * attn_cotangent.astype(jnp.float32)).astype(
        jnp.bfloat16
    )
    upstream = upstream.reshape(clip_count, frame_dev, positions, 1, model_width)
    packed = jnp.concatenate([projected, upstream], axis=3)
    received = lax.all_to_all(packed, "frame", split_axis=2, concat_axis=1, tiled=True)
    item_count = received.shape[0]
    frames = received.shape[1]
    across = received.shape[2]
    pieces = received.reshape(item_count, frames, across, 4, HEADS, HEAD_DIM)
    head_grads = attend_back(
        pieces[:, :, :, 0], pieces[:, :, :, 1], pieces[:, :, :, 2], pieces[:, :, :, 3]
    )
    stacked = jnp.stack(head_grads, axis=3).reshape(item_count, frames, across, 3, model_width)
    grad_projected = lax.all_to_all(stacked, "frame", split_axis=1, concat_axis=2, tiled=True)
    grad_rows = grad_projected.reshape(-1, 3 * model_width)
    device_count = lax.axis_size("frame") * lax.axis_size("space")
    grad_scale_factor = float(mod_rows.shape[0] * device_count) ** (-0.5)
    row_share = lax.psum_scatter(
        lax.dot_general(
            mod_rows, grad_rows, (((0,), (0,)), ((), ())), preferred_element_type=jnp.float32
        ).astype(jnp.bfloat16),
        "space",
        scatter_dimension=0,
        tiled=True,
    )
    grad_weight = lax.psum(row_share, "frame").astype(jnp.float32) * grad_scale_factor
    grad_hidden = lax.dot_general(
        grad_rows, w_full, (((1,), (1,)), ((), ())), preferred_element_type=jnp.float32
    )
    grad_hidden = grad_hidden.reshape(values_in.shape)
    local_sums = jnp.stack(
        [jnp.sum(grad_hidden, axis=(1, 2, 3)), jnp.sum(grad_hidden * normed, axis=(1, 2, 3))],
        axis=1,
    )
    grad_modulation = lax.psum(local_sums, ("frame", "space")) * grad_scale_factor
    grad_normed = grad_hidden * (1.0 + scale)
    grad_input = (
        grad_normed
        - jnp.mean(grad_normed, axis=-1, keepdims=True)
        - normed * jnp.mean(grad_normed * normed, axis=-1, keepdims=True)
    ) * inverse_std
    return (grad_input.astype(jnp.bfloat16), grad_weight, grad_modulation)


def solution(mesh):
    in_specs = (
        P(None, "frame", "space", None, None),
        P(None, "frame", "space", None, None),
        P("space", None),
        P(),
        P(),
        P(),
        P(),
    )
    out_specs = (P(None, "frame", "space", None, None), P("space", None), P())
    return jax.shard_map(
        per_device, mesh=mesh, in_specs=in_specs, out_specs=out_specs, check_vma=False
    )
```

profile of v0, /device:TPU:2, one launch (start us, length us, event | category | flops | bytes accessed | tf_op | source)
XLA Modules:
  0.0 491.3 jit_solution(7075564899825200032)
XLA Ops:
  7.2 0.7 all-gather.2.cloned.1.call-update
  8.6 2.9 gather_fusion
  11.6 0.7 compare_select_fusion
  12.9 1.2 multiply_convert_fusion.2
  15.6 49.8 %all-gather.2.cloned.1.call-done = bf16[1152,3456]{1,0:T(8,128)(2,1)} async-done(((bf16[72,3456]{1,0:T(8,128)(2,1)}), bf16[1152,3456]{1,0:T(8,128)(2,1)}) %all-gather.2.cloned.1.call-update) | async-done | bytes 7962640 | tf_op jit(solution)/shard_map/all_gather | solution.py:48
  65.5 7.1 %convolution_convert_fusion.1 = bf16[256,3456]{1,0:T(8,128)(2,1)} fusion(bf16[256,1152]{1,0:T(8,128)(2,1)S(1)} %bitcast.76, bf16[1152,3456]{1,0:T(8,128)(2,1)} %all-gather.2.cloned.1.call-done), kind=kOutput, calls=%fused_computation.3 | convolution fusion | flops 2039316480 | bytes 10321920 | tf_op jit(solution)/shard_map/dot_general | solution.py:49
  72.6 2.6 copy.63
  75.2 2.0 reshape.124
  77.2 4.6 pad_maximum_fusion
  81.8 4.9 copy.66
  86.7 67.7 %all_to_all.8 = bf16[2,1,128,4,1152]{4,3,1,0,2:T(4,128)(2,1)S(1)} all-to-all(bf16[2,1,128,4,1152]{4,3,1,0,2:T(4,128)(2,1)} %copy.66), channel_id=1, replica_groups=mesh['frame'=16,'space'=16] {'frame'}, dimensions={2} | all-to-all | bytes 4718592 | tf_op jit(solution)/shard_map/all_to_all | solution.py:57
  154.4 8.8 %reshape.148 = bf16[2,16,8,4,16,72]{5,4,3,0,2,1:T(8,128)(2,1)} reshape(bf16[2,1,128,4,1152]{4,3,1,0,2:T(4,128)(2,1)S(1)} %all_to_all.8) | data formatting | bytes 4718592 | tf_op jit(solution)/shard_map/reshape | solution.py:61
  163.2 3.6 fusion.25
  166.8 1.7 fusion.1
  168.5 1.8 multiply_reduce_fusion
  170.2 2.4 fusion.9
  172.7 2.2 fusion.10
  174.9 3.0 fusion.8
  178.2 1.5 stack.21
  180.0 1.3 stack.22
  181.4 1.5 copy.75
  182.9 1.3 stack.23
  184.6 40.6 %all_to_all.9 = bf16[2,16,8,3,1152]{4,2,0,3,1:T(8,128)(2,1)S(1)} all-to-all(bf16[2,16,8,3,1152]{4,2,0,3,1:T(8,128)(2,1)S(1)} %copy.76), channel_id=1, replica_groups=mesh['frame'=16,'space'=16] {'frame'}, dimensions={1} | all-to-all | bytes 3538944 | tf_op jit(solution)/shard_map/all_to_all | solution.py:66
  225.2 0.9 copy.77
  226.4 0.8 copy-done.4
  227.2 5.5 %convolution_convert_fusion = bf16[1152,3456]{1,0:T(8,128)(2,1)} fusion(bf16[256,1152]{1,0:T(8,128)(2,1)S(1)} %bitcast.77, bf16[256,3456]{1,0:T(8,128)(2,1)S(1)} %bitcast.73), kind=kOutput, calls=%fused_computation.2 | convolution fusion | flops 2042413056 | bytes 10321920 | tf_op jit(solution)/shard_map/dot_general | solution.py:71
  232.8 6.5 %fusion.19 = (f32[256]{0:T(256)}, f32[256,1152]{1,0:T(8,128)S(1)}) fusion(f32[2,1152]{1,0:T(2,128)S(1)} %bitcast.80, bf16[256,3456]{1,0:T(8,128)(2,1)S(1)} %bitcast.74, bf16[1152,3456]{1,0:T(8,128)(2,1)} %all-gather.2.cloned.1.call-done), kind=kOutput, calls=%fused_computation.34 | convolution fusion | flops 2039021312 | bytes 10921984 | tf_op jit(solution)/shard_map/dot_general | solution.py:79
  239.4 1.2 fusion.17
  240.6 77.9 %psum.15 = f32[2,2,1152]{2,0,1:T(2,128)S(1)} all-reduce(f32[2,2,1152]{2,0,1:T(2,128)S(1)} %pad_maximum_fusion.2), channel_id=1, replica_groups=mesh['frame'=16,'space'=16] {'frame','space'}, use_global_device_ids=true, to_apply=%region_10.0 | all-reduce | flops 4608 | bytes 36864 | tf_op jit(solution)/shard_map/psum | solution.py:87
  319.3 1.9 fusion.16
  321.2 161.5 %all-reduce.3.cloned.1.call-done = bf16[72,3456]{1,0:T(8,128)(2,1)} async-done(((bf16[72,3456]{1,0:T(8,128)(2,1)}), bf16[72,3456]{1,0:T(8,128)(2,1)}) %all-reduce.3.cloned.1.call-update) | async-done | bytes 497680 | tf_op jit(solution)/shard_map/psum | solution.py:78
  482.7 2.0 convert_multiply_fusion
  (50 shorter events, 4.9 us)
Async XLA Ops:
  7.2 5.1 %copy-start = (f32[1000]{0:T(1024)S(1)}, f32[1000]{0:T(1024)}, u32[]{:S(2)}) copy-start(f32[1000]{0:T(1024)} %param.11) | copy-start | bytes 12004
  7.2 7.6 %copy-start.2 = (bf16[2,1,2,64,1152]{4,3,2,1,0:T(8,128)(2,1)S(1)}, bf16[2,1,2,64,1152]{4,3,2,1,0:T(8,128)(2,1)}, u32[]{:S(2)}) copy-start(bf16[2,1,2,64,1152]{4,3,2,1,0:T(8,128)(2,1)} %param.7) | copy-start | bytes 1769476
  7.2 58.3 %all-gather.2.cloned.1.call-start = ((), (), s32[]{:S(2)}) async-start(), calls=%async_computation.3 | async-start | bytes 8460288 | tf_op jit(solution)/shard_map/all_gather | solution.py:48
  7.9 311.4 %reduce-scatter.5.cloned.1.call-start = ((), (), s32[]{:S(2)}) async-start(), calls=%async_computation.5 | async-start | bytes 8460288
  15.0 224.4 %copy-start.5 = (f32[2,2,64]{2,1,0:T(2,128)}, f32[2,2,64]{2,1,0:T(2,128)S(1)}, u32[]{:S(2)}) copy-start(f32[2,2,64]{2,1,0:T(2,128)S(1)} %broadcast_multiply_fusion.2) | copy-start | bytes 3076
  15.3 50.2 %copy-start.6 = (f32[2,2,64]{2,1,0:T(2,128)}, f32[2,2,64]{2,1,0:T(2,128)S(1)}, u32[]{:S(2)}) copy-start(f32[2,2,64]{2,1,0:T(2,128)S(1)} %add_rsqrt_fusion) | copy-start | bytes 3076
  15.6 49.8 %copy-start.3 = (bf16[2,1,2,64,1152]{4,3,2,1,0:T(8,128)(2,1)}, bf16[2,1,2,64,1152]{4,3,2,1,0:T(8,128)(2,1)S(1)}, u32[]{:S(2)}) copy-start(bf16[2,1,2,64,1152]{4,3,2,1,0:T(8,128)(2,1)S(1)} %fusion.12) | copy-start | bytes 1769476
  226.1 1.1 copy-start.4
  232.7 250.0 %all-reduce.3.cloned.1.call-start = ((), (), s32[]{:S(2)}) async-start(), calls=%async_computation.4 | async-start | bytes 995328 | tf_op jit(solution)/shard_map/psum | solution.py:78
  239.3 79.9 %copy-start.8 = (f32[256]{0:T(256)S(1)}, f32[256]{0:T(256)}, u32[]{:S(2)}) copy-start(f32[256]{0:T(256)} %get-tuple-element.25) | copy-start | bytes 3076
  239.4 79.9 %copy-start.7 = (f32[2,2,64]{2,1,0:T(2,128)S(1)}, f32[2,2,64]{2,1,0:T(2,128)}, u32[]{:S(2)}) copy-start(f32[2,2,64]{2,1,0:T(2,128)} %copy-done.6) | copy-start | bytes 3076
  319.3 165.5 %copy-start.1 = (f32[1000]{0:T(1024)S(1)}, f32[1000]{0:T(1024)}, u32[]{:S(2)}) copy-start(f32[1000]{0:T(1024)} %param.11) | copy-start | bytes 12004
Sparse Core Ops, SparseCore 0:
  9.9 55.5 all-gather.1
  232.9 74.6 reduce-scatter.4
  319.4 163.2 all-reduce.2
where the time goes:
time: 492 us; the launch traced here: 491 us
  waiting for transfers between devices  212 us (43%)
  blocking collectives  186 us (38%)
  local copies, waits for them, and re-layouts  35.1 us (7%)
  matrix products  30.3 us (6%)
  between operations  14 us (3%)
  other arithmetic  13.4 us (3%)
    psum x1, waiting for transfers between devices, per_device(): lax.psum(row_share, 'frame').astype(jnp.float32) * grad_scale_factor  162 us
    psum x1, blocking collectives, per_device(): lax.psum(local_sums, ('frame', 'space')) * grad_scale_factor  77.9 us
    all_to_all x1, blocking collectives, per_device(): lax.all_to_all(packed, 'frame', split_axis=2, concat_axis=1, tiled=True)  67.7 us
    all_gather x1, waiting for transfers between devices, per_device(): w_full = lax.all_gather(w_qkv, 'space', axis=0, tiled=True)  49.8 us
    all_to_all x1, blocking collectives, per_device(): lax.all_to_all(stacked, 'frame', split_axis=1, concat_axis=2, tiled=True)  40.6 us
  transfers between devices with their start and end apart: 3, of which 2 were waited for; matrix products, arithmetic and copies ran while one was open for 4% of the time, Pallas kernels for 0%

commit v1 on v0

--- a/solution.py
+++ b/solution.py
@@ -5,6 +5,11 @@
 
 HEADS = 16
 HEAD_DIM = 72
+
+
+def add_all(x, name):
+    parts = lax.all_gather(x, name)
+    return jnp.sum(parts, axis=0)
 
 
 def attend_back(queries, keys, values, upstream):
@@ -84,7 +89,7 @@
         [jnp.sum(grad_hidden, axis=(1, 2, 3)), jnp.sum(grad_hidden * normed, axis=(1, 2, 3))],
         axis=1,
     )
-    grad_modulation = lax.psum(local_sums, ("frame", "space")) * grad_scale_factor
+    grad_modulation = add_all(local_sums, ("frame", "space")) * grad_scale_factor
     grad_normed = grad_hidden * (1.0 + scale)
     grad_input = (
         grad_normed

time: 492 us -> 903 us (1.84)
  waiting for transfers between devices: 212 us -> 698 us
  blocking collectives: 186 us -> 108 us
    all_gather x0 -> x1, waiting for transfers between devices: none -> 419 us  [add_all(): parts = lax.all_gather(x, name)]
    psum x1 -> x0, blocking collectives: 77.9 us -> none  [per_device(): lax.psum(local_sums, ('frame', 'space')) * grad_scale_factor]
    unnamed x4 -> x5, waiting for transfers between devices: 0.72 us -> 67.3 us
  transfers between devices with their start and end apart: 3 -> 4, of which waited for: 2 -> 4; matrix products, arithmetic and copies ran while one was open for 4% -> 2% of each run, Pallas kernels for 0% -> 0%
where the time goes in v1:
time: 903 us
  waiting for transfers between devices  698 us (77%)
  blocking collectives  108 us (12%)
  local copies, waits for them, and re-layouts  34.5 us (4%)
  matrix products  30.3 us (3%)
  other arithmetic  17 us (2%)
  between operations  14 us (2%)
    all_gather x1, waiting for transfers between devices, add_all(): parts = lax.all_gather(x, name)  419 us
    psum x1, waiting for transfers between devices, per_device(): lax.psum(row_share, 'frame').astype(jnp.float32) * grad_scale_factor  162 us
    all_to_all x1, blocking collectives, per_device(): lax.all_to_all(packed, 'frame', split_axis=2, concat_axis=1, tiled=True)  67.7 us
    unnamed x5, waiting for transfers between devices  67.3 us
    all_gather x1, waiting for transfers between devices, per_device(): w_full = lax.all_gather(w_qkv, 'space', axis=0, tiled=True)  49.8 us
    all_to_all x1, blocking collectives, per_device(): lax.all_to_all(stacked, 'frame', split_axis=1, concat_axis=2, tiled=True)  40.6 us
  transfers between devices with their start and end apart: 4, of which 4 were waited for; matrix products, arithmetic and copies ran while one was open for 2% of the time, Pallas kernels for 0%

profile of v1, /device:TPU:2, one launch (start us, length us, event | category | flops | bytes accessed | tf_op | source)
XLA Modules:
  0.0 902.6 jit_solution(12030092307996121918)
XLA Ops:
  7.2 0.7 all-gather.4.cloned.1.call-update
  8.6 2.9 gather_fusion
  12.9 1.2 multiply_convert_fusion.2
  15.6 49.8 %all-gather.4.cloned.1.call-done = bf16[1152,3456]{1,0:T(8,128)(2,1)} async-done(((bf16[72,3456]{1,0:T(8,128)(2,1)}), bf16[1152,3456]{1,0:T(8,128)(2,1)}) %all-gather.4.cloned.1.call-update) | async-done | bytes 7962640 | tf_op jit(solution)/shard_map/all_gather | solution.py:53
  65.5 7.1 convolution_convert_fusion.1
  72.6 2.6 copy.60
  75.2 2.0 reshape.124
  77.2 4.6 pad_maximum_fusion
  81.8 4.9 copy.63
  86.7 67.7 %all_to_all.8 = bf16[2,1,128,4,1152]{4,3,1,0,2:T(4,128)(2,1)S(1)} all-to-all(bf16[2,1,128,4,1152]{4,3,1,0,2:T(4,128)(2,1)} %copy.63), channel_id=1, replica_groups=mesh['frame'=16,'space'=16] {'frame'}, dimensions={2} | all-to-all | bytes 4718592 | tf_op jit(solution)/shard_map/all_to_all | solution.py:62
  154.4 8.8 reshape.149
  163.2 3.6 fusion.25
  166.8 1.7 fusion.1
  168.5 1.8 multiply_reduce_fusion
  170.2 2.4 fusion.9
  172.7 2.2 fusion.10
  174.9 3.0 fusion.8
  178.2 1.5 stack.21
  180.0 1.3 stack.22
  181.4 1.5 copy.72
  182.9 1.3 stack.23
  184.6 40.6 %all_to_all.9 = bf16[2,16,8,3,1152]{4,2,0,3,1:T(8,128)(2,1)S(1)} all-to-all(bf16[2,16,8,3,1152]{4,2,0,3,1:T(8,128)(2,1)S(1)} %copy.73), channel_id=1, replica_groups=mesh['frame'=16,'space'=16] {'frame'}, dimensions={1} | all-to-all | bytes 3538944 | tf_op jit(solution)/shard_map/all_to_all | solution.py:71
  225.2 0.9 copy.74
  226.4 0.8 copy-done.4
  227.2 5.5 convolution_convert_fusion
  232.8 6.5 fusion.19
  240.7 66.6 %reduce-scatter.5.cloned.1.call-done = bf16[72,3456]{1,0:T(8,128)(2,1)} async-done(((bf16[1152,3456]{1,0:T(8,128)(2,1)}), bf16[72,3456]{1,0:T(8,128)(2,1)}) %reduce-scatter.5.cloned.1.call-update) | async-done | bytes 497680
  307.3 1.2 fusion.16
  308.6 419.0 %all-gather.6.cloned.1.call-done = f32[512,2,1152]{2,1,0:T(2,128)} async-done(((f32[2,2,1152]{2,1,0:T(2,128)}), f32[512,2,1152]{2,1,0:T(2,128)}) %all-gather.6.cloned.1.call-update) | async-done | bytes 4718608 | tf_op jit(solution)/shard_map/all_gather | solution.py:11
  727.6 3.7 reduce_sum.89
  731.9 162.2 %all-reduce.3.cloned.1.call-done = bf16[72,3456]{1,0:T(8,128)(2,1)} async-done(((bf16[72,3456]{1,0:T(8,128)(2,1)}), bf16[72,3456]{1,0:T(8,128)(2,1)}) %all-reduce.3.cloned.1.call-update) | async-done | bytes 497680 | tf_op jit(solution)/shard_map/psum | solution.py:83
  894.0 2.0 convert_multiply_fusion
  (54 shorter events, 6.7 us)
Async XLA Ops:
  7.2 5.1 copy-start
  7.2 7.6 copy-start.2
  7.2 58.3 %all-gather.4.cloned.1.call-start = ((), (), s32[]{:S(2)}) async-start(), calls=%async_computation.3 | async-start | bytes 8460288 | tf_op jit(solution)/shard_map/all_gather | solution.py:53
  7.9 299.3 %reduce-scatter.5.cloned.1.call-start = ((), (), s32[]{:S(2)}) async-start(), calls=%async_computation.6 | async-start | bytes 8460288
  15.3 50.2 %copy-start.5 = (f32[2,2,64]{2,1,0:T(2,128)}, f32[2,2,64]{2,1,0:T(2,128)S(1)}, u32[]{:S(2)}) copy-start(f32[2,2,64]{2,1,0:T(2,128)S(1)} %add_rsqrt_fusion) | copy-start | bytes 3076
  15.6 49.8 %copy-start.3 = (bf16[2,1,2,64,1152]{4,3,2,1,0:T(8,128)(2,1)}, bf16[2,1,2,64,1152]{4,3,2,1,0:T(8,128)(2,1)S(1)}, u32[]{:S(2)}) copy-start(bf16[2,1,2,64,1152]{4,3,2,1,0:T(8,128)(2,1)S(1)} %fusion.12) | copy-start | bytes 1769476
  226.1 1.1 copy-start.4
  232.7 494.8 %all-gather.6.cloned.1.call-start = ((), (), s32[]{:S(2)}) async-start(), calls=%async_computation.5 | async-start | bytes 4737024 | tf_op jit(solution)/shard_map/all_gather | solution.py:11
  232.8 6.5 copy-start.6
  239.3 1.3 copy-start.8
  239.3 68.0 %copy-start.7 = (f32[2,2,64]{2,1,0:T(2,128)S(1)}, f32[2,2,64]{2,1,0:T(2,128)}, u32[]{:S(2)}) copy-start(f32[2,2,64]{2,1,0:T(2,128)} %copy-done.5) | copy-start | bytes 3076
  240.5 653.5 %all-reduce.3.cloned.1.call-start = ((), (), s32[]{:S(2)}) async-start(), calls=%async_computation.4 | async-start | bytes 995328 | tf_op jit(solution)/shard_map/psum | solution.py:83
  727.6 168.5 %copy-start.1 = (f32[1000]{0:T(1024)S(1)}, f32[1000]{0:T(1024)}, u32[]{:S(2)}) copy-start(f32[1000]{0:T(1024)} %param.11) | copy-start | bytes 12004
Sparse Core Ops, SparseCore 0:
  9.9 55.5 all-gather.3
  232.9 74.3 reduce-scatter.4
  309.7 417.7 all-gather.5
  730.1 163.9 all-reduce.2
